TPU v7x, 32 devices: a whole 2x2x4 slice. The times are simulated.
32 devices in a mesh: ckpt: 1, vocab: 32 (over z, y, x, core).
Axes of the slice: x: 2, y: 2, z: 4, core: 2. Of those that a mesh axis runs over, the one named last changes fastest.
Arguments:
- hidden: bfloat16 [1, 512, 2048], P('ckpt', 'vocab'), may hold values from -16 to 16
- head: bfloat16 [1, 2048, 65536], P('ckpt', None, 'vocab'), may hold values from -1 to 1
- targets: int32 [512], replicated, may hold values from 0 to 65535
- segments: int32 [512], replicated, may hold values from 0 to 15, never falling along the last dimension, each value on 1 to 64 neighbouring positions
Outputs:
- scores: float32 [16], replicated
All inputs are finite; a program needn't handle non-finite values.
Results may differ from a plain program's by a relative error of at most 0.0003.
Values may be sent and summed in bfloat16 or wider, within the bound.
No kernel may reach another device: no remote copies, remote signals or barrier semaphores. Data moves between devices by JAX's collectives and lax.ppermute only.
A program may use at most 64 MiB of HBM per device.

v0:
```python
import jax
import jax.numpy as jnp
from jax import lax
from jax.sharding import PartitionSpec as P


def local_stats(token_rows, head_shard, wanted, offset):
    logits = jnp.dot(token_rows, head_shard, preferred_element_type=jnp.float32)
    maxima = jnp.max(logits, axis=1)
    expos = jnp.exp(logits - maxima[:, None])
    totals = jnp.sum(expos, axis=1)
    column = wanted - offset
    matches = lax.broadcasted_iota(jnp.int32, logits.shape, 1) == column[:, None]
    target_logit = jnp.sum(jnp.where(matches, logits, 0.0), axis=1)
    squares = jnp.sum(jnp.where(matches, 0.0, expos * expos), axis=1)
    return jnp.stack([maxima, totals, squares, target_logit])


def on_device(hidden, head, targets, segments):
    head_shard = head[0]
    local_rows = hidden[0]
    width = head_shard.shape[1]
    offset = lax.axis_index("vocab") * width
    gathered = lax.all_gather(local_rows, "vocab", axis=0, tiled=True)
    amount = gathered.shape[0]
    block = min(512, amount)

    def per_block(pair):
        return local_stats(pair[0], head_shard, pair[1], offset)

    stacked = lax.map(
        per_block,
        (
            gathered.reshape(amount // block, block, gathered.shape[1]),
            targets.reshape(amount // block, block),
        ),
    )
    stats = jnp.transpose(stacked, (1, 0, 2)).reshape(4, amount)
    maxima, totals, squares, target_logit = (stats[0], stats[1], stats[2], stats[3])
    top = lax.pmax(maxima, "vocab")
    factor = jnp.exp(maxima - top)
    totals, squares, target_logit = lax.psum(
        (totals * factor, squares * factor * factor, target_logit), "vocab"
    )
    maxima = top
    prob_target = jnp.exp(target_logit - maxima) / totals
    errors = jnp.sqrt((1.0 - prob_target) ** 2 + squares / (totals * totals))
    seq_count = targets.shape[0] // 32
    onehot = (
        lax.broadcasted_iota(jnp.int32, (seq_count, targets.shape[0]), 0) == segments[None, :]
    ).astype(jnp.float32)
    counts = jnp.sum(onehot, axis=1)
    means = jnp.dot(onehot, errors, precision=lax.Precision.HIGHEST) / counts
    return lax.psum(means, "ckpt")


def solution(mesh):
    placed = (P("ckpt", "vocab", None), P("ckpt", None, "vocab"), P(), P())
    return jax.shard_map(on_device, mesh=mesh, in_specs=placed, out_specs=P(), check_vma=False)
```

profile of v0, /device:TPU:0, one launch (start us, length us, event | category | flops | bytes accessed | tf_op | source)
XLA Modules:
  0.0 170.3 jit_solution(1786808813676618413)
XLA Ops:
  6.5 0.0 all-gather.3.cloned.1.call-start
  6.5 0.7 all-gather.3.cloned.1.call-update
  7.3 0.8 convert_reduce_fusion
  8.1 0.7 broadcast_subtract_fusion
  8.7 60.4 %all-gather.3.cloned.1.call-done = bf16[1,512,2048]{2,1,0:T(8,128)(2,1)} async-done(((bf16[1,16,2048]{2,1,0:T(8,128)(2,1)}), bf16[1,512,2048]{2,1,0:T(8,128)(2,1)}) %all-gather.3.cloned.1.call-update) | async-done | bytes 2097168 | tf_op jit(solution)/shard_map/all_gather | solution.py:24
  69.1 10.4 %fusion.7 = (f32[512]{0:T(512)S(1)}, f32[512,2048]{1,0:T(8,128)}) fusion(bf16[1,2048,2048]{2,1,0:T(8,128)(2,1)} %param.5, bf16[1,512,2048]{2,1,0:T(8,128)(2,1)} %all-gather.3.cloned.1.call-done), kind=kOutput, calls=%fused_computation.19 | convolution fusion | flops 4296015360 | bytes 14682112 | tf_op jit(solution)/shard_map/while/body/eval_jaxpr/dot_general | solution.py:8
  79.6 0.0 copy-start
  79.6 38.3 %pmax.7 = f32[512]{0:T(512)S(1)} all-reduce(f32[512]{0:T(512)S(1)} %get-tuple-element.31), channel_id=1, replica_groups=mesh['ckpt'=1,'vocab'=32] {'vocab'}, use_global_device_ids=true, to_apply=%region_3.4 | all-reduce | flops 512 | bytes 4096 | tf_op jit(solution)/shard_map/pmax | solution.py:40
  117.9 3.9 %select_reduce_fusion.1 = (f32[512]{0:T(512)S(1)}, f32[512]{0:T(512)S(1)}, f32[512]{0:T(512)S(1)}) fusion(f32[512,2048]{1,0:T(8,128)} %get-tuple-element.32, s32[512]{0:T(512)S(1)} %broadcast_subtract_fusion, f32[512]{0:T(512)S(1)} %get-tuple-element.31), kind=kLoop, calls=%fused_computation.4 | loop fusion | flops 8387072 | bytes 4204544 | tf_op jit(solution)/shard_map/while/body/eval_jaxpr/reduce_sum | solution.py:14
  121.8 40.9 %all-reduce = (f32[512]{0:T(512)S(1)}, f32[512]{0:T(512)S(1)}, f32[512]{0:T(512)S(1)}) all-reduce(f32[512]{0:T(512)S(1)} %get-tuple-element.30, f32[512]{0:T(512)S(1)} %get-tuple-element.29, f32[512]{0:T(512)S(1)} %get-tuple-element.15), channel_id=1, replica_groups=mesh['ckpt'=1,'vocab'=32] {'vocab'}, use_global_device_ids=true, to_apply=%region_7.8 | all-reduce | flops 1536 | bytes 12288 | tf_op jit(solution)/shard_map/psum | solution.py:42
  162.8 0.0 copy-done
  162.8 0.7 fusion.4
  (2 shorter events, 0.0 us)
Async XLA Ops:
  6.5 62.6 %all-gather.3.cloned.1.call-start = ((), (), s32[]{:S(2)}) async-start(), calls=%async_computation | async-start | bytes 2162688 | tf_op jit(solution)/shard_map/all_gather | solution.py:24
  79.6 83.2 %copy-start = (s32[512]{0:T(512)S(1)}, s32[512]{0:T(512)}, u32[]{:S(2)}) copy-start(s32[512]{0:T(512)} %param.7) | copy-start | bytes 6148
Sparse Core Ops, SparseCore 0:
  10.2 58.9 all-gather.2
where the time goes:
time: 171 us; the launch traced here: 170 us
  blocking collectives  79.3 us (46%)
  waiting for transfers between devices  61.1 us (36%)
  between operations  13.4 us (8%)
  matrix products  11.1 us (6%)
  other arithmetic  5.41 us (3%)
    all_gather x1, waiting for transfers between devices, on_device(): gathered = lax.all_gather(local_rows, 'vocab', axis=0, tiled=True)  60.4 us
    psum x1, blocking collectives, on_device(): lax.psum((totals * factor, squares * factor * factor, target_logit), 'voc...  40.9 us
    pmax x1, blocking collectives, on_device(): top = lax.pmax(maxima, 'vocab')  38.3 us
    dot_general x1, matrix products, local_stats(): logits = jnp.dot(token_rows, head_shard, preferred_element_type=jnp.float32)  10.4 us
    reduce_sum x1, other arithmetic, local_stats(): target_logit = jnp.sum(jnp.where(matches, logits, 0.0), axis=1)  3.9 us
  transfers between devices with their start and end apart: 1, of which 1 were waited for; matrix products, arithmetic and copies ran while one was open for 1% of the time, Pallas kernels for 0%

commit v1 on v0

v1 whole, which is shorter than its diff:
```python
import functools

import jax
import jax.numpy as jnp
from jax import lax
from jax.experimental import pallas as pl
from jax.experimental.pallas import tpu as pltpu
from jax.sharding import PartitionSpec as P

LANES = 128
STEP = 256
VMEM = pl.BlockSpec(memory_space=pltpu.VMEM)
SMEM = pl.BlockSpec(memory_space=pltpu.SMEM)
HBM = pl.BlockSpec(memory_space=pltpu.HBM)


def columns_of(order, me, wanted_ref, per, width, start, rows):
    blocks = [
        wanted_ref[pl.ds(pl.multiple_of((me ^ order[b]) * per, per), per), :]
        for b in range(start // per, (start + rows) // per)
    ]
    return jnp.concatenate(blocks, axis=0) - me * width


def row_stats(order, me, rows_ref, head_ref, wanted_ref, logits_ref, store, arrive=None):
    width = head_ref.shape[1]
    count = rows_ref.shape[0]
    per = count // len(order)
    largest = None
    for left in range(0, width, STEP):
        if arrive is not None:
            arrive(left // STEP)
        logits = jnp.dot(
            rows_ref[...], head_ref[:, pl.ds(left, STEP)], preferred_element_type=jnp.float32
        )
        logits_ref[:, pl.ds(left, STEP)] = logits
        for j in range(0, STEP, LANES):
            part = logits[:, j : j + LANES]
            largest = part if largest is None else jnp.maximum(largest, part)
    tops = jnp.max(largest, axis=1, keepdims=True)
    chunk = min(64, count)
    lane = lax.broadcasted_iota(jnp.int32, (chunk, LANES), 1)
    for start in range(0, count, chunk):
        rows = pl.ds(start, chunk)
        top = tops[start : start + chunk]
        column = columns_of(order, me, wanted_ref, per, width, start, chunk)
        total = jnp.zeros((chunk, LANES), jnp.float32)
        squares = jnp.zeros((chunk, LANES), jnp.float32)
        target = jnp.zeros((chunk, LANES), jnp.float32)
        for left in range(0, width, LANES):
            part = logits_ref[rows, pl.ds(left, LANES)]
            expo = jnp.exp(part - top)
            hit = lane == column - left
            total += expo
            squares += jnp.where(hit, 0.0, expo * expo)
            target += jnp.where(hit, part, 0.0)
        total = jnp.sum(total, axis=1, keepdims=True)
        squares = jnp.sum(squares, axis=1, keepdims=True)
        target = jnp.sum(target, axis=1, keepdims=True)
        packed = jnp.where(
            lane == 0, top, jnp.where(lane == 1, total, jnp.where(lane == 2, squares, target))
        )
        store(start, packed)


def first_kernel(order, me_ref, rows_ref, source_ref, wanted_ref, out_ref, head_ref, logits_ref, sems):
    def copy(tile):
        columns = pl.ds(tile * STEP, STEP)
        return pltpu.make_async_copy(source_ref.at[:, columns], head_ref.at[:, columns], sems.at[tile])

    for tile in range(head_ref.shape[1] // STEP):
        copy(tile).start()

    def store(start, packed):
        out_ref[pl.ds(start, packed.shape[0]), :] = packed

    row_stats(
        order, me_ref[0], rows_ref, head_ref, wanted_ref, logits_ref, store, lambda tile: copy(tile).wait()
    )


def middle_kernel(order, me_ref, rows_ref, head_ref, wanted_ref, out_ref, logits_ref):
    def store(start, packed):
        out_ref[pl.ds(start, packed.shape[0]), :] = packed

    row_stats(order, me_ref[0], rows_ref, head_ref, wanted_ref, logits_ref, store)


def last_kernel(
    order, first, middle, me_ref, rows_ref, head_ref, wanted_ref, first_ref, middle_ref, out_ref, logits_ref, placed_ref
):
    me = me_ref[0]
    per = rows_ref.shape[0] // len(order)

    def place(device, value):
        placed_ref[pl.ds(pl.multiple_of((me ^ device) * per, per), per), :] = value

    for devices, ref in ((first, first_ref), (middle, middle_ref)):
        for b, device in enumerate(devices):
            place(device, ref[pl.ds(b * per, per), :])

    def store(start, packed):
        for at in range(0, packed.shape[0], per):
            place(order[(start + at) // per], packed[at : at + per])

    row_stats(order, me, rows_ref, head_ref, wanted_ref, logits_ref, store)
    for start in range(0, placed_ref.shape[0], LANES):
        turned = jnp.transpose(placed_ref[pl.ds(start, LANES), :])
        out_ref[:, pl.ds(start, LANES)] = turned[:4]


def merge(mine, other):
    top = jnp.maximum(mine[0:1], other[0:1])
    scale = jnp.exp(mine[0:1] - top)
    other_scale = jnp.exp(other[0:1] - top)
    total = mine[1:2] * scale + other[1:2] * other_scale
    squares = mine[2:3] * (scale * scale) + other[2:3] * (other_scale * other_scale)
    return top, total, squares, mine[3:4] + other[3:4]


def merge_kernel(mine_ref, other_ref, out_ref):
    out_ref[...] = jnp.concatenate(merge(mine_ref[...], other_ref[...]), axis=0)


def final_kernel(mine_ref, other_ref, segments_ref, out_ref):
    top, total, squares, target = merge(mine_ref[...], other_ref[...])
    prob = jnp.exp(target - top) / total
    errors = jnp.sqrt((1.0 - prob) ** 2 + squares / (total * total))
    count = out_ref.shape[1]
    tokens = errors.shape[1]
    member = lax.broadcasted_iota(jnp.int32, (count, tokens), 0) == segments_ref[...]
    sums = jnp.sum(jnp.where(member, errors, 0.0), axis=1, keepdims=True)
    counts = jnp.sum(jnp.where(member, 1.0, 0.0), axis=1, keepdims=True)
    means = sums / counts
    diagonal = lax.broadcasted_iota(jnp.int32, (count, count), 0) == lax.broadcasted_iota(
        jnp.int32, (count, count), 1
    )
    out_ref[...] = jnp.sum(jnp.where(diagonal, means, 0.0), axis=0, keepdims=True)


def on_device(devices, hidden, head, targets, segments):
    def exchange(x, mask):
        return lax.ppermute(x, "vocab", [(i, i ^ mask) for i in range(devices)])

    rows, weights = hidden[0], head[0]
    per, depth = rows.shape
    width = weights.shape[1]
    tokens = per * devices
    me = lax.axis_index("vocab").astype(jnp.int32).reshape(1)
    wanted = jnp.broadcast_to(targets[:, None], (tokens, LANES))
    weights = pltpu.with_memory_space_constraint(weights, pltpu.HBM)

    def statistics(kernel, order, count, out_shape, scratch, *arrays):
        room = 4 * count * width + 2 * count * depth + 12 * tokens * LANES + (4 << 20)
        return pl.pallas_call(
            functools.partial(kernel, *order),
            out_shape=out_shape,
            in_specs=[SMEM] + [HBM if a is weights else VMEM for a in arrays],
            out_specs=jax.tree.map(lambda _: VMEM, out_shape),
            scratch_shapes=[pltpu.VMEM((count, width), jnp.float32)] + scratch,
            compiler_params=pltpu.CompilerParams(
                vmem_limit_bytes=room + (2 * depth * width if kernel is first_kernel else 0)
            ),
            cost_estimate=pl.CostEstimate(
                flops=2 * count * depth * width,
                bytes_accessed=2 * (count * depth + depth * width),
                transcendentals=count * width,
            ),
        )(me, *arrays)

    pieces, order, first = [rows], [0], None
    bit = devices // 2
    while bit > 1:
        masks = [bit // 2, bit, bit + bit // 2] if bit > 2 else [bit]
        rows = jnp.concatenate(pieces, axis=0)
        pieces = pieces + [exchange(rows, m) for m in masks]
        order = order + [m ^ o for m in masks for o in order]
        if first is None:
            first = tuple(order)
            pieces = [jnp.concatenate(pieces, axis=0)]
            first_other = exchange(pieces[0], 1)
            count = len(first) * per
            early, resident = statistics(
                first_kernel,
                (first,),
                count,
                (jax.ShapeDtypeStruct((count, LANES), jnp.float32), pltpu.VMEM(weights.shape, weights.dtype)),
                [pltpu.SemaphoreType.DMA((width // STEP,))],
                pieces[0],
                weights,
                wanted,
            )
        bit //= len(masks) + 1
    pieces, early, first_other = lax.optimization_barrier((pieces, early, first_other))
    middle_rows = jnp.concatenate(pieces[1:], axis=0)
    middle = tuple(order[len(first) :])
    middle_other = exchange(middle_rows, 1)
    count = len(middle) * per
    between = statistics(
        middle_kernel,
        (middle,),
        count,
        jax.ShapeDtypeStruct((count, LANES), jnp.float32),
        [],
        middle_rows,
        resident,
        wanted,
    )
    last = tuple(1 ^ o for o in first + middle)
    stats = statistics(
        last_kernel,
        (last, first, middle),
        len(last) * per,
        jax.ShapeDtypeStruct((4, tokens), jnp.float32),
        [pltpu.VMEM((tokens, LANES), jnp.float32)],
        jnp.concatenate([first_other, middle_other], axis=0),
        resident,
        wanted,
        early,
        between,
    )

    small = pltpu.CompilerParams(vmem_limit_bytes=2 << 20)
    masks = [1]
    while 2 * (masks[-1] & ~1 or 1) < devices:
        masks.append(2 * (masks[-1] & ~1 or 1) | 1)
    for mask in masks[:-1]:
        stats = pl.pallas_call(
            merge_kernel,
            out_shape=jax.ShapeDtypeStruct(stats.shape, jnp.float32),
            in_specs=[VMEM, VMEM],
            out_specs=VMEM,
            compiler_params=small,
        )(stats, exchange(stats, mask))
    means = pl.pallas_call(
        final_kernel,
        out_shape=jax.ShapeDtypeStruct((1, tokens // 32), jnp.float32),
        in_specs=[VMEM, VMEM, VMEM],
        out_specs=VMEM,
        compiler_params=small,
    )(stats, exchange(stats, masks[-1]), segments[None, :])
    return lax.psum(means[0], "ckpt")


def solution(mesh):
    placed = (P("ckpt", "vocab", None), P("ckpt", None, "vocab"), P(), P())
    body = functools.partial(on_device, mesh.shape["vocab"])
    return jax.shard_map(body, mesh=mesh, in_specs=placed, out_specs=P(), check_vma=False)
```

time: 171 us -> 49.1 us (0.29)
  blocking collectives: 79.3 us -> 0 us
  waiting for transfers between devices: 61.1 us -> 19.9 us
  starting transfers between devices: 0.01 us -> 15.5 us
  between operations: 13.4 us -> 0.12 us
  Pallas kernels: 0 us -> 11.6 us
  matrix products: 11.1 us -> 0 us
  other arithmetic: 5.41 us -> 0.97 us
    all_gather x1 -> x0, waiting for transfers between devices: 60.4 us -> none  [on_device(): gathered = lax.all_gather(local_rows, 'vocab', axis=0, tiled=True)]
    psum x1 -> x0, blocking collectives: 40.9 us -> none  [on_device(): lax.psum((totals * factor, squares * factor * factor, target_logit), 'voc...]
    pmax x1 -> x0, blocking collectives: 38.3 us -> none  [on_device(): top = lax.pmax(maxima, 'vocab')]
    ppermute x0 -> x13, waiting for transfers between devices: none -> 19.9 us  [exchange(): return lax.ppermute(x, 'vocab', [(i, i ^ mask) for i in range(devices)])]
    ppermute x0 -> x13, starting transfers between devices: none -> 15.5 us  [exchange(): return lax.ppermute(x, 'vocab', [(i, i ^ mask) for i in range(devices)])]
    pallas_call x0 -> x8, Pallas kernels: none -> 11.6 us  [the longest x3 10.9 us: statistics(): pl.pallas_call(functools.partial(kernel, *order), out_shape=out_shape, in...]
    dot_general x2 -> x0, matrix products: 11.1 us -> none  [the longest x1 10.4 us: local_stats(): logits = jnp.dot(token_rows, head_shard, preferred_element_type=jnp.float32)]
    reduce_sum x2 -> x0, other arithmetic: 4.7 us -> none  [the longest x1 3.9 us: local_stats(): target_logit = jnp.sum(jnp.where(matches, logits, 0.0), axis=1)]
  transfers between devices with their start and end apart: 1 -> 13, of which waited for: 1 -> 10; matrix products, arithmetic and copies ran while one was open for 1% -> 2% of each run, Pallas kernels for 0% -> 15%
where the time goes in v1:
time: 49.1 us; the launch traced here: 48.9 us
  waiting for transfers between devices  19.9 us (41%)
  starting transfers between devices  15.5 us (32%)
  Pallas kernels  11.6 us (24%)
  other arithmetic  0.97 us (2%)
  local copies, waits for them, and re-layouts  0.86 us (2%)
    ppermute x13, waiting for transfers between devices, exchange(): return lax.ppermute(x, 'vocab', [(i, i ^ mask) for i in range(devices)])  19.9 us
    ppermute x13, starting transfers between devices, exchange(): return lax.ppermute(x, 'vocab', [(i, i ^ mask) for i in range(devices)])  15.5 us
    pallas_call x3, Pallas kernels, statistics(): pl.pallas_call(functools.partial(kernel, *order), out_shape=out_shape, in...  10.9 us
  transfers between devices with their start and end apart: 13, of which 10 were waited for; matrix products, arithmetic and copies ran while one was open for 2% of the time, Pallas kernels for 15%

profile of v1, /device:TPU:0, one launch (start us, length us, event | category | flops | bytes accessed | tf_op | source)
XLA Modules:
  0.0 48.9 jit_solution(4462113406252267496)
XLA Ops:
  0.0 5.1 %collective-permute-start.2 = (bf16[16,2048]{1,0:T(8,128)(2,1)}, bf16[16,2048]{1,0:T(8,128)(2,1)S(1)}, u32[]{:S(2)}, u32[]{:S(2)}) collective-permute-start(bf16[16,2048]{1,0:T(8,128)(2,1)} %bitcast.7), channel_id=1, source_target_pairs={{0,24},{1,25},{2,26},{3,27},{4,28},{5,29},{6,30},{7,31},{8,16},{9,... | collective-permute-start | bytes 196616 | tf_op jit(solution)/shard_map/ppermute | solution.py:143
  5.1 0.0 collective-permute-start.1
  5.1 0.6 %collective-permute-start = (bf16[16,2048]{1,0:T(8,128)(2,1)}, bf16[16,2048]{1,0:T(8,128)(2,1)S(1)}, u32[]{:S(2)}, u32[]{:S(2)}) collective-permute-start(bf16[16,2048]{1,0:T(8,128)(2,1)} %bitcast.9), channel_id=1, source_target_pairs={{0,8},{1,9},{2,10},{3,11},{4,12},{5,13},{6,14},{7,15},{8,0},{9,1},... | collective-permute-start | bytes 196616 | tf_op jit(solution)/shard_map/ppermute | solution.py:143
  5.6 2.2 %collective-permute-done.2 = bf16[16,2048]{1,0:T(8,128)(2,1)S(1)} collective-permute-done((bf16[16,2048]{1,0:T(8,128)(2,1)}, bf16[16,2048]{1,0:T(8,128)(2,1)S(1)}, u32[]{:S(2)}, u32[]{:S(2)}) %collective-permute-start.2) | collective-permute-done | bytes 65568 | tf_op jit(solution)/shard_map/ppermute | solution.py:143
  7.9 3.0 %collective-permute-done.1 = bf16[16,2048]{1,0:T(8,128)(2,1)S(1)} collective-permute-done((bf16[16,2048]{1,0:T(8,128)(2,1)}, bf16[16,2048]{1,0:T(8,128)(2,1)S(1)}, u32[]{:S(2)}, u32[]{:S(2)}) %collective-permute-start.1) | collective-permute-done | bytes 65568 | tf_op jit(solution)/shard_map/ppermute | solution.py:143
  10.9 0.0 collective-permute-done
  10.9 0.9 %pad_maximum_fusion.1.rows_ref = bf16[64,2048]{1,0:T(8,128)(2,1)S(1)} fusion(bf16[16,2048]{1,0:T(8,128)(2,1)S(1)} %collective-permute-done.2, bf16[16,2048]{1,0:T(8,128)(2,1)S(1)} %collective-permute-done.1, bf16[16,2048]{1,0:T(8,128)(2,1)S(1)} %collective-permute-done, bf16[16,2048]{1,0:T(8,128)(2,1)} %bitcast.10), kind=kLoop, calls=%fused_computation.1 | loop fusion | flops 1048576 | bytes 524288 | tf_op jit(solution)/shard_map/concatenate | solution.py:180
  11.8 0.1 collective-permute-start.6
  11.8 2.5 %collective-permute-start.5 = (bf16[64,2048]{1,0:T(8,128)(2,1)S(1)}, bf16[64,2048]{1,0:T(8,128)(2,1)S(1)}, u32[]{:S(2)}, u32[]{:S(2)}) collective-permute-start(bf16[64,2048]{1,0:T(8,128)(2,1)S(1)} %pad_maximum_fusion.1.rows_ref), channel_id=1, source_target_pairs={{0,6},{1,7},{2,4},{3,5},{4,2},{5,3},{6,0},{7,1},{8,14},{9,15},{10,... | collective-permute-start | bytes 786440 | tf_op jit(solution)/shard_map/ppermute | solution.py:143
  14.3 0.5 %collective-permute-start.4 = (bf16[64,2048]{1,0:T(8,128)(2,1)S(1)}, bf16[64,2048]{1,0:T(8,128)(2,1)S(1)}, u32[]{:S(2)}, u32[]{:S(2)}) collective-permute-start(bf16[64,2048]{1,0:T(8,128)(2,1)S(1)} %pad_maximum_fusion.1.rows_ref), channel_id=1, source_target_pairs={{0,4},{1,5},{2,6},{3,7},{4,0},{5,1},{6,2},{7,3},{8,12},{9,13},{10,... | collective-permute-start | bytes 786440 | tf_op jit(solution)/shard_map/ppermute | solution.py:143
  14.9 0.5 %collective-permute-start.3 = (bf16[64,2048]{1,0:T(8,128)(2,1)S(1)}, bf16[64,2048]{1,0:T(8,128)(2,1)S(1)}, u32[]{:S(2)}, u32[]{:S(2)}) collective-permute-start(bf16[64,2048]{1,0:T(8,128)(2,1)S(1)} %pad_maximum_fusion.1.rows_ref), channel_id=1, source_target_pairs={{0,2},{1,3},{2,0},{3,1},{4,6},{5,7},{6,4},{7,5},{8,10},{9,11},{10,... | collective-permute-start | bytes 786440 | tf_op jit(solution)/shard_map/ppermute | solution.py:143
  15.4 0.8 %broadcast_in_dim.4.wanted_ref = s32[512,128]{1,0:T(8,128)S(1)} broadcast(s32[512]{0:T(512)} %param.6), dimensions={0} | broadcast | bytes 264192 | tf_op jit(solution)/shard_map/broadcast_in_dim | solution.py:150
  16.2 5.0 %shard_map.46 = (f32[64,128]{1,0:T(8,128)S(1)}, bf16[2048,2048]{1,0:T(8,128)(2,1)S(1)}) custom-call(s32[1]{0:T(128)} %bitcast.me_ref, bf16[64,2048]{1,0:T(8,128)(2,1)S(1)} %pad_maximum_fusion.1.rows_ref, bf16[2048,2048]{1,0:T(8,128)(2,1)} %bitcast.6, s32[512,128]{1,0:T(8,128)S(1)} %broadcast_in_dim.4.wanted_ref), custom_call_target="tpu_custom_call" | custom-call | flops 536870912 | bytes 8650752 | tf_op jit(solution)/shard_map/pallas_call | solution.py:155
  21.2 0.0 collective-permute-done.6
  21.2 0.8 %collective-permute-done.5 = bf16[64,2048]{1,0:T(8,128)(2,1)S(1)} collective-permute-done((bf16[64,2048]{1,0:T(8,128)(2,1)S(1)}, bf16[64,2048]{1,0:T(8,128)(2,1)S(1)}, u32[]{:S(2)}, u32[]{:S(2)}) %collective-permute-start.5) | collective-permute-done | bytes 262176 | tf_op jit(solution)/shard_map/ppermute | solution.py:143
  22.0 5.0 %collective-permute-done.4 = bf16[64,2048]{1,0:T(8,128)(2,1)S(1)} collective-permute-done((bf16[64,2048]{1,0:T(8,128)(2,1)S(1)}, bf16[64,2048]{1,0:T(8,128)(2,1)S(1)}, u32[]{:S(2)}, u32[]{:S(2)}) %collective-permute-start.4) | collective-permute-done | bytes 262176 | tf_op jit(solution)/shard_map/ppermute | solution.py:143
  27.1 0.1 collective-permute-done.3
  27.2 0.1 collective-permute-start.7
  27.3 2.6 %shard_map.47.middle_ref = f32[192,128]{1,0:T(8,128)S(1)} custom-call(s32[1]{0:T(128)} %bitcast.me_ref, bf16[192,2048]{1,0:T(8,128)(2,1)S(1)} %constant_dynamic-update-slice_fusion.rows_ref, bf16[2048,2048]{1,0:T(8,128)(2,1)S(1)} %get-tuple-element.17.head_ref, s32[512,128]{1,0:T(8,128)S(1)} %broadcast_in_dim.4.wanted_ref), custom_call_target="tpu_custom_call" | custom-call | flops 1610612736 | bytes 9175040 | tf_op jit(solution)/shard_map/pallas_call | solution.py:155
  29.9 0.0 collective-permute-done.7
  29.9 0.1 pad_maximum_fusion.rows_ref
  30.0 0.0 copy-start
  30.0 3.3 %shard_map.48.mine_ref = f32[4,512]{1,0:T(4,128)S(1)} custom-call(s32[1]{0:T(128)} %bitcast.me_ref, bf16[256,2048]{1,0:T(8,128)(2,1)S(1)} %pad_maximum_fusion.rows_ref, bf16[2048,2048]{1,0:T(8,128)(2,1)S(1)} %get-tuple-element.17.head_ref, s32[512,128]{1,0:T(8,128)S(1)} %broadcast_in_dim.4.wanted_ref, f32[64,128]{1,0:T(8,128)S(1)} %get-tuple-element.18.first_ref, ...), custom_call_target="tpu_custom_call" | custom-call | flops 2147483648 | bytes 9437184 | tf_op jit(solution)/shard_map/pallas_call | solution.py:155
  33.3 0.5 %collective-permute-start.8 = (f32[4,512]{1,0:T(4,128)S(1)}, f32[4,512]{1,0:T(4,128)S(1)}, u32[]{:S(2)}, u32[]{:S(2)}) collective-permute-start(f32[4,512]{1,0:T(4,128)S(1)} %shard_map.48.mine_ref), channel_id=1, source_target_pairs={{0,1},{1,0},{2,3},{3,2},{4,5},{5,4},{6,7},{7,6},{8,9},{9,8},{10,11... | collective-permute-start | bytes 24584 | tf_op jit(solution)/shard_map/ppermute | solution.py:143
  33.9 0.8 %collective-permute-done.8.other_ref = f32[4,512]{1,0:T(4,128)S(1)} collective-permute-done((f32[4,512]{1,0:T(4,128)S(1)}, f32[4,512]{1,0:T(4,128)S(1)}, u32[]{:S(2)}, u32[]{:S(2)}) %collective-permute-start.8) | collective-permute-done | bytes 8224 | tf_op jit(solution)/shard_map/ppermute | solution.py:143
  34.7 1.5 %collective-permute-start.9 = (f32[4,512]{1,0:T(4,128)S(1)}, f32[4,512]{1,0:T(4,128)S(1)}, u32[]{:S(2)}, u32[]{:S(2)}) collective-permute-start(f32[4,512]{1,0:T(4,128)S(1)} %shard_map.49.mine_ref), channel_id=1, source_target_pairs={{0,3},{1,2},{2,1},{3,0},{4,7},{5,6},{6,5},{7,4},{8,11},{9,10},{10,... | collective-permute-start | bytes 24584 | tf_op jit(solution)/shard_map/ppermute | solution.py:143
  36.2 1.7 %collective-permute-done.9.other_ref = f32[4,512]{1,0:T(4,128)S(1)} collective-permute-done((f32[4,512]{1,0:T(4,128)S(1)}, f32[4,512]{1,0:T(4,128)S(1)}, u32[]{:S(2)}, u32[]{:S(2)}) %collective-permute-start.9) | collective-permute-done | bytes 8224 | tf_op jit(solution)/shard_map/ppermute | solution.py:143
  37.9 1.4 %collective-permute-start.10 = (f32[4,512]{1,0:T(4,128)S(1)}, f32[4,512]{1,0:T(4,128)S(1)}, u32[]{:S(2)}, u32[]{:S(2)}) collective-permute-start(f32[4,512]{1,0:T(4,128)S(1)} %shard_map.50.mine_ref), channel_id=1, source_target_pairs={{0,5},{1,4},{2,7},{3,6},{4,1},{5,0},{6,3},{7,2},{8,13},{9,12},{10,... | collective-permute-start | bytes 24584 | tf_op jit(solution)/shard_map/ppermute | solution.py:143
  39.3 1.7 %collective-permute-done.10.other_ref = f32[4,512]{1,0:T(4,128)S(1)} collective-permute-done((f32[4,512]{1,0:T(4,128)S(1)}, f32[4,512]{1,0:T(4,128)S(1)}, u32[]{:S(2)}, u32[]{:S(2)}) %collective-permute-start.10) | collective-permute-done | bytes 8224 | tf_op jit(solution)/shard_map/ppermute | solution.py:143
  41.1 1.1 %collective-permute-start.11 = (f32[4,512]{1,0:T(4,128)S(1)}, f32[4,512]{1,0:T(4,128)S(1)}, u32[]{:S(2)}, u32[]{:S(2)}) collective-permute-start(f32[4,512]{1,0:T(4,128)S(1)} %shard_map.51.mine_ref), channel_id=1, source_target_pairs={{0,9},{1,8},{2,11},{3,10},{4,13},{5,12},{6,15},{7,14},{8,1},{9,0},... | collective-permute-start | bytes 24584 | tf_op jit(solution)/shard_map/ppermute | solution.py:143
  42.1 2.1 %collective-permute-done.11.other_ref = f32[4,512]{1,0:T(4,128)S(1)} collective-permute-done((f32[4,512]{1,0:T(4,128)S(1)}, f32[4,512]{1,0:T(4,128)S(1)}, u32[]{:S(2)}, u32[]{:S(2)}) %collective-permute-start.11) | collective-permute-done | bytes 8224 | tf_op jit(solution)/shard_map/ppermute | solution.py:143
  44.2 1.6 %collective-permute-start.12 = (f32[4,512]{1,0:T(4,128)S(1)}, f32[4,512]{1,0:T(4,128)S(1)}, u32[]{:S(2)}, u32[]{:S(2)}) collective-permute-start(f32[4,512]{1,0:T(4,128)S(1)} %shard_map.52.mine_ref), channel_id=1, source_target_pairs={{0,17},{1,16},{2,19},{3,18},{4,21},{5,20},{6,23},{7,22},{8,25},{9,... | collective-permute-start | bytes 24584 | tf_op jit(solution)/shard_map/ppermute | solution.py:143
  45.8 2.5 %collective-permute-done.12.other_ref = f32[4,512]{1,0:T(4,128)S(1)} collective-permute-done((f32[4,512]{1,0:T(4,128)S(1)}, f32[4,512]{1,0:T(4,128)S(1)}, u32[]{:S(2)}, u32[]{:S(2)}) %collective-permute-start.12) | collective-permute-done | bytes 8224 | tf_op jit(solution)/shard_map/ppermute | solution.py:143
  48.3 0.0 copy-done
  48.3 0.6 %shard_map.53 = f32[1,16]{1,0:T(1,128)} custom-call(f32[4,512]{1,0:T(4,128)S(1)} %shard_map.52.mine_ref, f32[4,512]{1,0:T(4,128)S(1)} %collective-permute-done.12.other_ref, s32[1,512]{1,0:T(1,128)S(1)} %bitcast.5), custom_call_target="tpu_custom_call" | custom-call | tf_op jit(solution)/shard_map/pallas_call | solution.py:235
  (7 shorter events, 0.1 us)
Async XLA Ops:
  0.0 7.9 %collective-permute-start.2 = (bf16[16,2048]{1,0:T(8,128)(2,1)}, bf16[16,2048]{1,0:T(8,128)(2,1)S(1)}, u32[]{:S(2)}, u32[]{:S(2)}) collective-permute-start(bf16[16,2048]{1,0:T(8,128)(2,1)} %bitcast.7), channel_id=1, source_target_pairs={{0,24},{1,25},{2,26},{3,27},{4,28},{5,29},{6,30},{7,31},{8,16},{9,... | collective-permute-start | bytes 196616 | tf_op jit(solution)/shard_map/ppermute | solution.py:143
  5.1 5.8 %collective-permute-start.1 = (bf16[16,2048]{1,0:T(8,128)(2,1)}, bf16[16,2048]{1,0:T(8,128)(2,1)S(1)}, u32[]{:S(2)}, u32[]{:S(2)}) collective-permute-start(bf16[16,2048]{1,0:T(8,128)(2,1)} %bitcast.8), channel_id=1, source_target_pairs={{0,16},{1,17},{2,18},{3,19},{4,20},{5,21},{6,22},{7,23},{8,24},{9,... | collective-permute-start | bytes 196616 | tf_op jit(solution)/shard_map/ppermute | solution.py:143
  5.1 5.8 %collective-permute-start = (bf16[16,2048]{1,0:T(8,128)(2,1)}, bf16[16,2048]{1,0:T(8,128)(2,1)S(1)}, u32[]{:S(2)}, u32[]{:S(2)}) collective-permute-start(bf16[16,2048]{1,0:T(8,128)(2,1)} %bitcast.9), channel_id=1, source_target_pairs={{0,8},{1,9},{2,10},{3,11},{4,12},{5,13},{6,14},{7,15},{8,0},{9,1},... | collective-permute-start | bytes 196616 | tf_op jit(solution)/shard_map/ppermute | solution.py:143
  11.8 9.4 %collective-permute-start.6 = (bf16[64,2048]{1,0:T(8,128)(2,1)S(1)}, bf16[64,2048]{1,0:T(8,128)(2,1)S(1)}, u32[]{:S(2)}, u32[]{:S(2)}) collective-permute-start(bf16[64,2048]{1,0:T(8,128)(2,1)S(1)} %pad_maximum_fusion.1.rows_ref), channel_id=1, source_target_pairs={{0,1},{1,0},{2,3},{3,2},{4,5},{5,4},{6,7},{7,6},{8,9},{9,8},{10,11... | collective-permute-start | bytes 786440 | tf_op jit(solution)/shard_map/ppermute | solution.py:143
  11.8 10.2 %collective-permute-start.5 = (bf16[64,2048]{1,0:T(8,128)(2,1)S(1)}, bf16[64,2048]{1,0:T(8,128)(2,1)S(1)}, u32[]{:S(2)}, u32[]{:S(2)}) collective-permute-start(bf16[64,2048]{1,0:T(8,128)(2,1)S(1)} %pad_maximum_fusion.1.rows_ref), channel_id=1, source_target_pairs={{0,6},{1,7},{2,4},{3,5},{4,2},{5,3},{6,0},{7,1},{8,14},{9,15},{10,... | collective-permute-start | bytes 786440 | tf_op jit(solution)/shard_map/ppermute | solution.py:143
  14.3 12.7 %collective-permute-start.4 = (bf16[64,2048]{1,0:T(8,128)(2,1)S(1)}, bf16[64,2048]{1,0:T(8,128)(2,1)S(1)}, u32[]{:S(2)}, u32[]{:S(2)}) collective-permute-start(bf16[64,2048]{1,0:T(8,128)(2,1)S(1)} %pad_maximum_fusion.1.rows_ref), channel_id=1, source_target_pairs={{0,4},{1,5},{2,6},{3,7},{4,0},{5,1},{6,2},{7,3},{8,12},{9,13},{10,... | collective-permute-start | bytes 786440 | tf_op jit(solution)/shard_map/ppermute | solution.py:143
  14.9 12.3 %collective-permute-start.3 = (bf16[64,2048]{1,0:T(8,128)(2,1)S(1)}, bf16[64,2048]{1,0:T(8,128)(2,1)S(1)}, u32[]{:S(2)}, u32[]{:S(2)}) collective-permute-start(bf16[64,2048]{1,0:T(8,128)(2,1)S(1)} %pad_maximum_fusion.1.rows_ref), channel_id=1, source_target_pairs={{0,2},{1,3},{2,0},{3,1},{4,6},{5,7},{6,4},{7,5},{8,10},{9,11},{10,... | collective-permute-start | bytes 786440 | tf_op jit(solution)/shard_map/ppermute | solution.py:143
  27.2 2.6 %collective-permute-start.7 = (bf16[192,2048]{1,0:T(8,128)(2,1)S(1)}, bf16[192,2048]{1,0:T(8,128)(2,1)S(1)}, u32[]{:S(2)}, u32[]{:S(2)}) collective-permute-start(bf16[192,2048]{1,0:T(8,128)(2,1)S(1)} %constant_dynamic-update-slice_fusion.rows_ref), channel_id=1, source_target_pairs={{0,1},{1,0},{2,3},{3,2},{4,5},{5,4},{6,7},{7,6},{8,9},{9,8},{10,11... | collective-permute-start | bytes 2359304 | tf_op jit(solution)/shard_map/ppermute | solution.py:143
  30.0 18.3 %copy-start = (s32[512]{0:T(512)S(1)}, s32[512]{0:T(512)}, u32[]{:S(2)}) copy-start(s32[512]{0:T(512)} %param.7) | copy-start | bytes 6148
  33.3 1.4 %collective-permute-start.8 = (f32[4,512]{1,0:T(4,128)S(1)}, f32[4,512]{1,0:T(4,128)S(1)}, u32[]{:S(2)}, u32[]{:S(2)}) collective-permute-start(f32[4,512]{1,0:T(4,128)S(1)} %shard_map.48.mine_ref), channel_id=1, source_target_pairs={{0,1},{1,0},{2,3},{3,2},{4,5},{5,4},{6,7},{7,6},{8,9},{9,8},{10,11... | collective-permute-start | bytes 24584 | tf_op jit(solution)/shard_map/ppermute | solution.py:143
  34.7 3.1 %collective-permute-start.9 = (f32[4,512]{1,0:T(4,128)S(1)}, f32[4,512]{1,0:T(4,128)S(1)}, u32[]{:S(2)}, u32[]{:S(2)}) collective-permute-start(f32[4,512]{1,0:T(4,128)S(1)} %shard_map.49.mine_ref), channel_id=1, source_target_pairs={{0,3},{1,2},{2,1},{3,0},{4,7},{5,6},{6,5},{7,4},{8,11},{9,10},{10,... | collective-permute-start | bytes 24584 | tf_op jit(solution)/shard_map/ppermute | solution.py:143
  37.9 3.1 %collective-permute-start.10 = (f32[4,512]{1,0:T(4,128)S(1)}, f32[4,512]{1,0:T(4,128)S(1)}, u32[]{:S(2)}, u32[]{:S(2)}) collective-permute-start(f32[4,512]{1,0:T(4,128)S(1)} %shard_map.50.mine_ref), channel_id=1, source_target_pairs={{0,5},{1,4},{2,7},{3,6},{4,1},{5,0},{6,3},{7,2},{8,13},{9,12},{10,... | collective-permute-start | bytes 24584 | tf_op jit(solution)/shard_map/ppermute | solution.py:143
  41.1 3.1 %collective-permute-start.11 = (f32[4,512]{1,0:T(4,128)S(1)}, f32[4,512]{1,0:T(4,128)S(1)}, u32[]{:S(2)}, u32[]{:S(2)}) collective-permute-start(f32[4,512]{1,0:T(4,128)S(1)} %shard_map.51.mine_ref), channel_id=1, source_target_pairs={{0,9},{1,8},{2,11},{3,10},{4,13},{5,12},{6,15},{7,14},{8,1},{9,0},... | collective-permute-start | bytes 24584 | tf_op jit(solution)/shard_map/ppermute | solution.py:143
  44.2 4.0 %collective-permute-start.12 = (f32[4,512]{1,0:T(4,128)S(1)}, f32[4,512]{1,0:T(4,128)S(1)}, u32[]{:S(2)}, u32[]{:S(2)}) collective-permute-start(f32[4,512]{1,0:T(4,128)S(1)} %shard_map.52.mine_ref), channel_id=1, source_target_pairs={{0,17},{1,16},{2,19},{3,18},{4,21},{5,20},{6,23},{7,22},{8,25},{9,... | collective-permute-start | bytes 24584 | tf_op jit(solution)/shard_map/ppermute | solution.py:143
